TPU v7x, 32 devices: a whole 2x2x4 slice. The times are simulated.
32 devices in a mesh: grp: 2 (over x), ctg: 16 (over z, y, core).
Axes of the slice: x: 2, y: 2, z: 4, core: 2. Of those that a mesh axis runs over, the one named last changes fastest.
Arguments:
- flow_tiles: bfloat16 [128, 256, 3072], P('ctg'), may hold values from -0.109375 to 0.109375
- tile_pattern: int32 [128, 2, 24], P('ctg'), may hold values 0 or 1
- monitored: int32 [128, 256], P('ctg'), may hold values from 0 to 16383
- ratings: float32 [16384], replicated, may hold values from 0.3 to 3
- base_flow: float32 [64, 128, 256], P('grp', 'ctg'), parts along dimension 0, may hold values from -6 to 6
- unit_cost: float32 [64, 3072], P(('grp', 'ctg')), parts along dimension 0, may hold values from -6 to 6
- unit_floor: float32 [3072], replicated, may hold values from 0 to 0.5
- unit_span: float32 [3072], replicated, may hold values from 0.5 to 2
- ramp_limit: float32 [3072], replicated, may hold values from 0.05 to 0.5
- ramp_mask: int32 [3072], replicated, may hold values 0 or 1
- demand: float32 [64], P(('grp', 'ctg')), parts along dimension 0, may hold values from 1228.8 to 2457.6
- start_output: float32 [64, 3072], P(('grp', 'ctg')), parts along dimension 0, may hold values from 0 to 1.5
- start_flow_dual: float32 [64, 128, 256], P('grp', 'ctg'), parts along dimension 0, may hold values from -2 to 2
- start_ramp_dual: float32 [64, 3072], P(('grp', 'ctg')), parts along dimension 0, may hold values from -3 to 3
Outputs:
- output_levels: float32 [64, 3072], P(('grp', 'ctg')), parts along dimension 0
- flow_dual: float32 [64, 128, 256], P('grp', 'ctg'), parts along dimension 0
- ramp_dual: float32 [64, 3072], P(('grp', 'ctg')), parts along dimension 0
- balance_price: float32 [64], P(('grp', 'ctg')), parts along dimension 0
There are 2 independent parts, one for each index of `grp`. A program takes and returns all parts, laid end to end along the dimension named above; an argument that names none is the same for every part. Nothing has to cross between parts.
All inputs are finite; a program needn't handle non-finite values. No bound on the sum of `tile_pattern` on one device may be relied on, other than what follows from the above.
Results may differ from a plain program's by a relative error of at most 0.0045.
Values may be sent and summed in bfloat16 or wider, within the bound.
A program may use at most 128 MiB of HBM per device.

v0:
```python
import math
import jax
import jax.numpy as jnp
from jax import lax
from jax.sharding import PartitionSpec as P

ITERS = 4


def mask_tiles(flow_tiles, tile_pattern):
    ctg_count, line_count, unit_count = flow_tiles.shape
    blocks = flow_tiles.reshape(ctg_count, line_count // 128, 128, unit_count // 128, 128)
    gates = tile_pattern.astype(jnp.bfloat16)[:, :, None, :, None]
    return (blocks * gates).reshape(ctg_count, line_count, unit_count)


def dual_prox(trial, dual_step, lower_side, upper_side):
    return trial - dual_step * jnp.clip(trial / dual_step, lower_side, upper_side)


def body(
    flow_tiles,
    tile_pattern,
    monitored,
    ratings,
    base_flow,
    unit_cost,
    unit_floor,
    unit_span,
    ramp_limit,
    ramp_mask,
    demand,
    start_output,
    start_flow_dual,
    start_ramp_dual,
):
    ctg_count, line_count, unit_count = flow_tiles.shape
    devices = lax.axis_size("ctg")
    position = lax.axis_index("ctg")
    masked = mask_tiles(flow_tiles, tile_pattern)
    flow_limit = ratings[monitored]
    flow_lower = base_flow - flow_limit[None]
    flow_upper = base_flow + flow_limit[None]
    step_size = 0.5 / (2.0 + math.sqrt(ctg_count * devices * line_count / unit_count))
    balance = 1.0 / math.sqrt(unit_count)
    ceiling = unit_floor + unit_span
    ramp_on = ramp_mask.astype(jnp.float32)
    weight = jnp.float32(1.0)
    hour_rows = start_output.shape[0]
    zero_row = jnp.zeros((1, unit_count), jnp.float32)
    flow_dual = start_flow_dual
    levels, costs, ramp_dual, demands = (
        lax.all_gather(start_output, "ctg", axis=0, tiled=True),
        lax.all_gather(unit_cost, "ctg", axis=0, tiled=True),
        lax.all_gather(start_ramp_dual, "ctg", axis=0, tiled=True),
        lax.all_gather(demand, "ctg", axis=0, tiled=True),
    )
    balance_price = jnp.zeros(demands.shape, jnp.float32)
    for iteration in range(ITERS):
        primal_step = step_size / weight
        dual_step = step_size * weight
        dual_half = flow_dual.astype(jnp.bfloat16)
        own_term = jnp.einsum("tkm,kmu->tu", dual_half, masked, preferred_element_type=jnp.float32)
        pulled = lax.psum(own_term.astype(jnp.bfloat16), "ctg").astype(jnp.float32)
        before = jnp.concatenate([zero_row, ramp_dual[:-1]], axis=0)
        gradient = (
            costs + pulled + ramp_on * (before - ramp_dual) + balance * balance_price[:, None]
        )
        moved = jnp.clip(levels - primal_step * gradient, unit_floor, ceiling)
        extended = 2.0 * moved - levels
        extended_half = extended.astype(jnp.bfloat16)
        flows = jnp.einsum("kmu,tu->tkm", masked, extended_half, preferred_element_type=jnp.float32)
        dual_new = dual_prox(flow_dual + dual_step * flows, dual_step, flow_lower, flow_upper)
        change = ramp_on * jnp.concatenate([extended[1:] - extended[:-1], zero_row], axis=0)
        ramp_new = dual_prox(ramp_dual + dual_step * change, dual_step, -ramp_limit, ramp_limit)
        balance_row = balance * (jnp.sum(extended, axis=1) - demands)
        price_new = balance_price + dual_step * balance_row
        if iteration < ITERS - 1:
            primal_sq = jnp.sum((moved - levels) ** 2)
            flow_sq = lax.psum(jnp.sum((dual_new - flow_dual) ** 2), "ctg")
            dual_sq = (
                flow_sq
                + jnp.sum((ramp_new - ramp_dual) ** 2)
                + jnp.sum((price_new - balance_price) ** 2)
            )
            weight = jnp.sqrt(weight) * ((dual_sq + 1e-06) / (primal_sq + 1e-06)) ** 0.25
        levels = moved
        flow_dual = dual_new
        ramp_dual = ramp_new
        balance_price = price_new
    first_hour = position * hour_rows
    own_levels = lax.dynamic_slice_in_dim(levels, first_hour, hour_rows, 0)
    own_ramp = lax.dynamic_slice_in_dim(ramp_dual, first_hour, hour_rows, 0)
    own_price = lax.dynamic_slice_in_dim(balance_price, first_hour, hour_rows, 0)
    return (own_levels, flow_dual, own_ramp, own_price)


def solution(mesh):
    return jax.shard_map(
        body,
        mesh=mesh,
        in_specs=(
            P("ctg", None, None),
            P("ctg", None, None),
            P("ctg", None),
            P(),
            P("grp", "ctg", None),
            P(("grp", "ctg"), None),
            P(),
            P(),
            P(),
            P(),
            P(("grp", "ctg")),
            P(("grp", "ctg"), None),
            P("grp", "ctg", None),
            P(("grp", "ctg"), None),
        ),
        out_specs=(
            P(("grp", "ctg"), None),
            P("grp", "ctg", None),
            P(("grp", "ctg"), None),
            P(("grp", "ctg")),
        ),
        check_vma=False,
    )
```

profile of v0, /device:TPU:0, one launch (start us, length us, event | category | flops | bytes accessed | tf_op | source)
XLA Modules:
  0.0 492.0 jit_solution(2523741557012118708)
XLA Ops:
  7.9 6.3 %mul.232 = bf16[8,2,128,24,128]{4,3,2,1,0:T(8,128)(2,1)} broadcast(bf16[8,2,24]{2,1,0:T(2,128)(2,1)S(1)} %convert_element_type.57), dimensions={0,1,3} | broadcast | bytes 12583680 | tf_op jit(solution)/shard_map/mul | solution.py:14
  14.2 19.3 %mul.233 = bf16[8,256,3072]{2,1,0:T(8,128)(2,1)} reshape(bf16[8,2,128,24,128]{4,3,2,1,0:T(8,128)(2,1)} %mul.232) | data formatting | bytes 25165824 | tf_op jit(solution)/shard_map/mul | solution.py:14
  33.5 11.4 %mul.234 = bf16[8,256,3072]{2,1,0:T(8,128)(2,1)S(1)} multiply(bf16[8,256,3072]{2,1,0:T(8,128)(2,1)} %param.14, bf16[8,256,3072]{2,1,0:T(8,128)(2,1)} %mul.233) | non-fusion elementwise | flops 6291456 | bytes 37748736 | tf_op jit(solution)/shard_map/mul | solution.py:14
  45.0 4.6 copy-done.1
  49.7 2.9 fusion.4
  52.7 24.2 %all-gather.1 = f32[16,2,3072]{2,1,0:T(2,128)S(1)} all-gather(f32[1,2,3072]{2,1,0:T(2,128)S(1)} %bitcast.64), channel_id=1, replica_groups=mesh['grp'=2,'ctg'=16] {'ctg'}, dimensions={0}, use_global_device_ids=true | all-gather | bytes 417792 | tf_op jit(solution)/shard_map/all_gather | solution.py:54
  77.2 18.6 %all-gather.2 = f32[16,2,3072]{2,1,0:T(2,128)S(1)} all-gather(f32[1,2,3072]{2,1,0:T(2,128)S(1)} %bitcast.65), channel_id=1, replica_groups=mesh['grp'=2,'ctg'=16] {'ctg'}, dimensions={0}, use_global_device_ids=true | all-gather | bytes 417792 | tf_op jit(solution)/shard_map/all_gather | solution.py:55
  96.2 20.1 %all-gather = f32[16,2,3072]{2,1,0:T(2,128)S(1)} all-gather(f32[1,2,3072]{2,1,0:T(2,128)S(1)} %bitcast.66), channel_id=1, replica_groups=mesh['grp'=2,'ctg'=16] {'ctg'}, dimensions={0}, use_global_device_ids=true | all-gather | bytes 417792 | tf_op jit(solution)/shard_map/all_gather | solution.py:53
  116.6 11.8 %gather_fusion = f32[2048]{0:T(1024)S(1)} fusion(f32[16384]{0:T(1024)S(1)} %copy-done, s32[2048]{0:T(1024)S(1)} %broadcast_clamp_fusion), kind=kCustom, calls=%fused_computation | custom fusion | bytes 24576 | tf_op jit(solution)/shard_map/gather | solution.py:41
  129.9 16.5 %all-reduce.15.cloned.1.call-done = bf16[32,3072]{1,0:T(8,128)(2,1)} async-done(((bf16[32,3072]{1,0:T(8,128)(2,1)}), bf16[32,3072]{1,0:T(8,128)(2,1)}) %all-reduce.15.cloned.1.call-update) | async-done | bytes 196624 | tf_op jit(solution)/shard_map/psum | solution.py:64
  148.4 9.1 %multiply_reduce_fusion.8 = (f32[]{:T(128)}, f32[32,8,256]{2,0,1:T(8,128)S(1)}) fusion(f32[32,8,256]{2,1,0:T(8,128)S(1)} %copy-done.3, f32[8,256]{1,0:T(8,128)S(1)} %reshape.25, f32[32,8,256]{2,1,0:T(8,128)S(1)} %copy-done.2, bf16[8,256,3072]{2,1,0:T(8,128)(2,1)} %copy-done.1, f32[32,3072]{1,0:T(8,128)S(1)} %get-tuple-element.42), kind=kOutput, calls=%fused_computation.47 | convolution fusion | flops 403537920 | bytes 13770756 | tf_op jit(solution)/shard_map/kmu,tu->tkm/dot_general | solution.py:72
  157.5 7.5 %fusion = bf16[32,3072]{1,0:T(8,128)(2,1)} fusion(bf16[8,256,3072]{2,1,0:T(8,128)(2,1)} %copy-done.1, f32[32,8,256]{2,0,1:T(8,128)S(1)} %get-tuple-element.46, f32[32,8,256]{2,1,0:T(8,128)S(1)} %copy-done.2, f32[8,256]{1,0:T(8,128)S(1)} %reshape.25), kind=kOutput, calls=%fused_computation.5 | convolution fusion | flops 403275776 | bytes 13312000 | tf_op jit(solution)/shard_map/tkm,kmu->tu/dot_general | solution.py:63
  165.1 31.2 %all-reduce.9 = (f32[32]{0:T(128)S(1)}, f32[]{:T(128)}) all-reduce(f32[32]{0:T(128)S(1)} %dynamic-update-slice, f32[]{:T(128)} %get-tuple-element.45), channel_id=1, replica_groups=mesh['grp'=2,'ctg'=16] {'ctg'}, use_global_device_ids=true, to_apply=%add.8 | all-reduce | flops 33 | bytes 264
  200.3 54.7 %all-reduce.17.cloned.1.call-done = bf16[32,3072]{1,0:T(8,128)(2,1)} async-done(((bf16[32,3072]{1,0:T(8,128)(2,1)}), bf16[32,3072]{1,0:T(8,128)(2,1)}) %all-reduce.17.cloned.1.call-update) | async-done | bytes 196624 | tf_op jit(solution)/shard_map/psum | solution.py:64
  255.1 1.7 multiply_reduce_fusion.2
  257.0 9.1 %multiply_reduce_fusion.7 = (f32[]{:T(128)}, f32[32,8,256]{2,0,1:T(8,128)S(1)}) fusion(f32[32,8,256]{2,0,1:T(8,128)S(1)} %get-tuple-element.46, f32[]{:T(128)S(6)} %mul.251, f32[8,256]{1,0:T(8,128)S(1)} %reshape.25, f32[32,8,256]{2,1,0:T(8,128)S(1)} %copy-done.2, bf16[8,256,3072]{2,1,0:T(8,128)(2,1)} %copy-done.1, f32[32,3072]{1,0:T(8,128)S(1)} %get-tuple-element.36), kind=kOutput, calls=%fused_computation.44 | convolution fusion | flops 403865600 | bytes 13770760 | tf_op jit(solution)/shard_map/kmu,tu->tkm/dot_general | solution.py:72
  266.8 7.5 %fusion.1 = bf16[32,3072]{1,0:T(8,128)(2,1)} fusion(bf16[8,256,3072]{2,1,0:T(8,128)(2,1)} %copy-done.1, f32[32,8,256]{2,0,1:T(8,128)S(1)} %get-tuple-element.48, f32[]{:T(128)S(6)} %mul.251, f32[32,8,256]{2,1,0:T(8,128)S(1)} %copy-done.2, f32[8,256]{1,0:T(8,128)S(1)} %reshape.25), kind=kOutput, calls=%fused_computation.6 | convolution fusion | flops 403275776 | bytes 13312004 | tf_op jit(solution)/shard_map/tkm,kmu->tu/dot_general | solution.py:63
  275.0 31.3 %psum.52 = f32[]{:T(128)} all-reduce(f32[]{:T(128)} %get-tuple-element.47), channel_id=1, replica_groups=mesh['grp'=2,'ctg'=16] {'ctg'}, use_global_device_ids=true, to_apply=%region_9.10 | all-reduce | flops 1 | bytes 8 | tf_op jit(solution)/shard_map/psum | solution.py:80
  309.1 55.2 %all-reduce.19.cloned.1.call-done = bf16[32,3072]{1,0:T(8,128)(2,1)} async-done(((bf16[32,3072]{1,0:T(8,128)(2,1)}), bf16[32,3072]{1,0:T(8,128)(2,1)}) %all-reduce.19.cloned.1.call-update) | async-done | bytes 196624 | tf_op jit(solution)/shard_map/psum | solution.py:64
  366.3 9.1 %multiply_reduce_fusion.6 = (f32[]{:T(128)}, f32[32,8,256]{2,0,1:T(8,128)S(1)}) fusion(f32[32,8,256]{2,0,1:T(8,128)S(1)} %get-tuple-element.48, f32[]{:T(128)S(6)} %mul.268, f32[]{:T(128)S(6)} %mul.251, f32[8,256]{1,0:T(8,128)S(1)} %reshape.25, f32[32,8,256]{2,1,0:T(8,128)S(1)} %copy-done.2, bf16[8,256,3072]{2,1,0:T(8,128)(2,1)} %copy-done.1, ...), kind=kOutput, calls=%fused_computation.41 | convolution fusion | flops 403865600 | bytes 13770764 | tf_op jit(solution)/shard_map/kmu,tu->tkm/dot_general | solution.py:72
  376.1 7.5 %fusion.2 = bf16[32,3072]{1,0:T(8,128)(2,1)} fusion(bf16[8,256,3072]{2,1,0:T(8,128)(2,1)} %copy-done.1, f32[32,8,256]{2,0,1:T(8,128)S(1)} %get-tuple-element.50, f32[]{:T(128)S(6)} %mul.268, f32[32,8,256]{2,1,0:T(8,128)S(1)} %copy-done.2, f32[8,256]{1,0:T(8,128)S(1)} %reshape.25), kind=kOutput, calls=%fused_computation.7 | convolution fusion | flops 403275776 | bytes 13312004 | tf_op jit(solution)/shard_map/tkm,kmu->tu/dot_general | solution.py:63
  384.2 31.1 %psum.54 = f32[]{:T(128)} all-reduce(f32[]{:T(128)} %get-tuple-element.49), channel_id=1, replica_groups=mesh['grp'=2,'ctg'=16] {'ctg'}, use_global_device_ids=true, to_apply=%region_16.17 | all-reduce | flops 1 | bytes 8 | tf_op jit(solution)/shard_map/psum | solution.py:80
  418.0 55.5 %all-reduce.21.cloned.1.call-done = bf16[32,3072]{1,0:T(8,128)(2,1)} async-done(((bf16[32,3072]{1,0:T(8,128)(2,1)}), bf16[32,3072]{1,0:T(8,128)(2,1)}) %all-reduce.21.cloned.1.call-update) | async-done | bytes 196624 | tf_op jit(solution)/shard_map/psum | solution.py:64
  474.9 8.4 %multiply_subtract_fusion.7 = f32[32,8,256]{2,0,1:T(8,128)S(1)} fusion(bf16[8,256,3072]{2,1,0:T(8,128)(2,1)} %copy-done.1, f32[32,8,256]{2,0,1:T(8,128)S(1)} %get-tuple-element.50, f32[32,3072]{1,0:T(8,128)S(1)} %get-tuple-element.19, f32[]{:T(128)S(6)} %mul.286, f32[]{:T(128)S(6)} %mul.268, f32[8,256]{1,0:T(8,128)S(1)} %reshape.25, ...), kind=kOutput, calls=%fused_computation.40 | convolution fusion | flops 403668992 | bytes 13770760 | tf_op jit(solution)/shard_map/kmu,tu->tkm/dot_general | solution.py:72
  (73 shorter events, 14.3 us)
Async XLA Ops:
  7.2 109.4 %copy-start = (f32[16384]{0:T(1024)S(1)}, f32[16384]{0:T(1024)}, u32[]{:S(2)}) copy-start(f32[16384]{0:T(1024)} %param.17) | copy-start | bytes 196612
  7.2 139.3 %all-reduce.15.cloned.1.call-start = ((), (), s32[]{:S(2)}) async-start(), calls=%async_computation | async-start | bytes 393216 | tf_op jit(solution)/shard_map/psum | solution.py:64
  14.2 19.3 %copy-start.3 = (f32[32,8,256]{2,1,0:T(8,128)S(1)}, f32[32,8,256]{2,1,0:T(8,128)}, u32[]{:S(2)}) copy-start(f32[32,8,256]{2,1,0:T(8,128)} %param.26) | copy-start | bytes 786436
  45.0 4.6 copy-start.1
  49.6 3.1 copy-start.9
  49.6 3.1 copy-start.6
  49.6 27.6 %copy-start.7 = (f32[2,3072]{1,0:T(2,128)S(1)}, f32[2,3072]{1,0:T(2,128)}, u32[]{:S(2)}) copy-start(f32[2,3072]{1,0:T(2,128)} %param.27) | copy-start | bytes 73732
  49.6 46.5 %copy-start.11 = (s32[8,256]{1,0:T(8,128)S(1)}, s32[8,256]{1,0:T(8,128)}, u32[]{:S(2)}) copy-start(s32[8,256]{1,0:T(8,128)} %param.16) | copy-start | bytes 24580
  49.6 46.6 %copy-start.8 = (f32[2,3072]{1,0:T(2,128)S(1)}, f32[2,3072]{1,0:T(2,128)}, u32[]{:S(2)}) copy-start(f32[2,3072]{1,0:T(2,128)} %param.25) | copy-start | bytes 73732
  49.6 78.8 %copy-start.5 = (f32[3072]{0:T(1024)S(1)}, f32[3072]{0:T(1024)}, u32[]{:S(2)}) copy-start(f32[3072]{0:T(1024)} %param.22) | copy-start | bytes 36868
  49.6 78.8 %copy-start.4 = (f32[3072]{0:T(1024)S(1)}, f32[3072]{0:T(1024)}, u32[]{:S(2)}) copy-start(f32[3072]{0:T(1024)} %param.20) | copy-start | bytes 36868
  49.6 78.8 %copy-start.10 = (f32[3072]{0:T(1024)S(1)}, f32[3072]{0:T(1024)}, u32[]{:S(2)}) copy-start(f32[3072]{0:T(1024)} %param.21) | copy-start | bytes 36868
  49.6 78.8 %copy-start.13 = (u32[32]{0:T(128)S(1)}, u32[32]{0:T(128)}, u32[]{:S(2)}) copy-start(u32[32]{0:T(128)} %constant.69) | copy-start | bytes 388
  49.6 80.0 %copy-start.12 = (f32[2]{0:T(128)S(1)}, f32[2]{0:T(128)}, u32[]{:S(2)}) copy-start(f32[2]{0:T(128)} %param.24) | copy-start | bytes 28
  49.7 98.7 %copy-start.2 = (f32[32,8,256]{2,1,0:T(8,128)S(1)}, f32[32,8,256]{2,1,0:T(8,128)}, u32[]{:S(2)}) copy-start(f32[32,8,256]{2,1,0:T(8,128)} %param.18) | copy-start | bytes 786436
  52.6 202.4 %all-reduce.17.cloned.1.call-start = ((), (), s32[]{:S(2)}) async-start(), calls=%async_computation.1 | async-start | bytes 393216 | tf_op jit(solution)/shard_map/psum | solution.py:64
  165.0 199.3 %all-reduce.19.cloned.1.call-start = ((), (), s32[]{:S(2)}) async-start(), calls=%async_computation.2 | async-start | bytes 393216 | tf_op jit(solution)/shard_map/psum | solution.py:64
  274.3 199.3 %all-reduce.21.cloned.1.call-start = ((), (), s32[]{:S(2)}) async-start(), calls=%async_computation.3 | async-start | bytes 393216 | tf_op jit(solution)/shard_map/psum | solution.py:64
Sparse Core Ops, SparseCore 0:
  52.8 93.6 all-reduce.14
  165.2 89.8 all-reduce.16
  274.5 89.8 all-reduce.18
  383.7 89.8 all-reduce.20
where the time goes:
time: 493 us; the launch traced here: 492 us
  waiting for transfers between devices  182 us (37%)
  blocking collectives  157 us (32%)
  matrix products  61 us (12%)
  local copies, waits for them, and re-layouts  45.1 us (9%)
  other arithmetic  24.1 us (5%)
  between operations  23 us (5%)
    psum x4, waiting for transfers between devices, body(): pulled = lax.psum(own_term.astype(jnp.bfloat16), 'ctg').astype(jnp.float32)  182 us
    psum x2, blocking collectives, body(): flow_sq = lax.psum(jnp.sum((dual_new - flow_dual) ** 2), 'ctg')  62.5 us
    dot_general x4, matrix products, body(): jnp.einsum('kmu,tu->tkm', masked, extended_half, preferred_element_type=j...  35.6 us
    unnamed x1, blocking collectives  31.2 us
    mul x2, local copies, waits for them, and re-layouts, mask_tiles(): return (blocks * gates).reshape(ctg_count, line_count, unit_count)  25.6 us
    dot_general x4, matrix products, body(): jnp.einsum('tkm,kmu->tu', dual_half, masked, preferred_element_type=jnp.f...  25.4 us
    all_gather x1, blocking collectives, body(): lax.all_gather(unit_cost, 'ctg', axis=0, tiled=True)  24.2 us
    all_gather x1, blocking collectives, body(): lax.all_gather(start_output, 'ctg', axis=0, tiled=True)  20.1 us
  transfers between devices with their start and end apart: 4, of which 4 were waited for; matrix products, arithmetic and copies ran while one was open for 3% of the time, Pallas kernels for 0%

commit v1 on v0

--- a/solution.py
+++ b/solution.py
@@ -61,7 +61,9 @@
         dual_step = step_size * weight
         dual_half = flow_dual.astype(jnp.bfloat16)
         own_term = jnp.einsum("tkm,kmu->tu", dual_half, masked, preferred_element_type=jnp.float32)
-        pulled = lax.psum(own_term.astype(jnp.bfloat16), "ctg").astype(jnp.float32)
+        pulled = jnp.sum(lax.all_gather(own_term.astype(jnp.bfloat16), "ctg"), 0).astype(
+            jnp.float32
+        )
         before = jnp.concatenate([zero_row, ramp_dual[:-1]], axis=0)
         gradient = (
             costs + pulled + ramp_on * (before - ramp_dual) + balance * balance_price[:, None]

time: 493 us -> 343 us (0.70)
  waiting for transfers between devices: 182 us -> 21 us
  other arithmetic: 24.1 us -> 30.5 us
    psum x4 -> x0, waiting for transfers between devices: 182 us -> none  [body(): pulled = lax.psum(own_term.astype(jnp.bfloat16), 'ctg').astype(jnp.float32)]
    all_gather x0 -> x4, waiting for transfers between devices: none -> 20.9 us  [body(): lax.all_gather(own_term.astype(jnp.bfloat16), 'ctg')]
    reduce_sum x0 -> x4, other arithmetic: none -> 9.96 us  [body(): jnp.sum(lax.all_gather(own_term.astype(jnp.bfloat16), 'ctg'), 0)]
  transfers between devices with their start and end apart: 4 -> 4, of which waited for: 4 -> 3; matrix products, arithmetic and copies ran while one was open for 3% -> 5% of each run, Pallas kernels for 0% -> 0%
where the time goes in v1:
time: 343 us; the launch traced here: 342 us
  blocking collectives  161 us (47%)
  matrix products  61 us (18%)
  local copies, waits for them, and re-layouts  45.1 us (13%)
  other arithmetic  30.5 us (9%)
  between operations  23.1 us (7%)
  waiting for transfers between devices  21 us (6%)
    psum x2, blocking collectives, body(): flow_sq = lax.psum(jnp.sum((dual_new - flow_dual) ** 2), 'ctg')  64.5 us
    dot_general x4, matrix products, body(): jnp.einsum('kmu,tu->tkm', masked, extended_half, preferred_element_type=j...  35.6 us
    unnamed x1, blocking collectives  31.3 us
    mul x2, local copies, waits for them, and re-layouts, mask_tiles(): return (blocks * gates).reshape(ctg_count, line_count, unit_count)  25.6 us
    dot_general x4, matrix products, body(): jnp.einsum('tkm,kmu->tu', dual_half, masked, preferred_element_type=jnp.f...  25.4 us
    all_gather x1, blocking collectives, body(): lax.all_gather(unit_cost, 'ctg', axis=0, tiled=True)  24.7 us
    all_gather x1, blocking collectives, body(): lax.all_gather(start_output, 'ctg', axis=0, tiled=True)  21.3 us
    all_gather x4, waiting for transfers between devices, body(): lax.all_gather(own_term.astype(jnp.bfloat16), 'ctg')  20.9 us
  transfers between devices with their start and end apart: 4, of which 3 were waited for; matrix products, arithmetic and copies ran while one was open for 5% of the time, Pallas kernels for 0%

profile of v1, /device:TPU:0, one launch (start us, length us, event | category | flops | bytes accessed | tf_op | source)
XLA Modules:
  0.0 341.7 jit_solution(2142437732403663585)
XLA Ops:
  7.9 6.3 %mul.232 = bf16[8,2,128,24,128]{4,3,2,1,0:T(8,128)(2,1)} broadcast(bf16[8,2,24]{2,1,0:T(2,128)(2,1)S(1)} %convert_element_type.65), dimensions={0,1,3} | broadcast | bytes 12583680 | tf_op jit(solution)/shard_map/mul | solution.py:14
  14.2 19.3 %mul.233 = bf16[8,256,3072]{2,1,0:T(8,128)(2,1)} reshape(bf16[8,2,128,24,128]{4,3,2,1,0:T(8,128)(2,1)} %mul.232) | data formatting | bytes 25165824 | tf_op jit(solution)/shard_map/mul | solution.py:14
  33.5 11.4 %mul.234 = bf16[8,256,3072]{2,1,0:T(8,128)(2,1)S(1)} multiply(bf16[8,256,3072]{2,1,0:T(8,128)(2,1)} %param.14, bf16[8,256,3072]{2,1,0:T(8,128)(2,1)} %mul.233) | non-fusion elementwise | flops 6291456 | bytes 37748736 | tf_op jit(solution)/shard_map/mul | solution.py:14
  45.0 4.6 %copy-done.2 = bf16[8,256,3072]{2,1,0:T(8,128)(2,1)} copy-done((bf16[8,256,3072]{2,1,0:T(8,128)(2,1)}, bf16[8,256,3072]{2,1,0:T(8,128)(2,1)S(1)}, u32[]{:S(2)}) %copy-start.2) | copy-done | bytes 12582936
  49.6 2.9 fusion.4
  52.7 24.7 %all-gather.5 = f32[16,2,3072]{2,1,0:T(2,128)S(1)} all-gather(f32[1,2,3072]{2,1,0:T(2,128)S(1)} %bitcast.72), channel_id=1, replica_groups=mesh['grp'=2,'ctg'=16] {'ctg'}, dimensions={0}, use_global_device_ids=true | all-gather | bytes 417792 | tf_op jit(solution)/shard_map/all_gather | solution.py:54
  77.7 19.0 %all-gather.6 = f32[16,2,3072]{2,1,0:T(2,128)S(1)} all-gather(f32[1,2,3072]{2,1,0:T(2,128)S(1)} %bitcast.73), channel_id=1, replica_groups=mesh['grp'=2,'ctg'=16] {'ctg'}, dimensions={0}, use_global_device_ids=true | all-gather | bytes 417792 | tf_op jit(solution)/shard_map/all_gather | solution.py:55
  97.0 21.3 %all-gather.4 = f32[16,2,3072]{2,1,0:T(2,128)S(1)} all-gather(f32[1,2,3072]{2,1,0:T(2,128)S(1)} %bitcast.74), channel_id=1, replica_groups=mesh['grp'=2,'ctg'=16] {'ctg'}, dimensions={0}, use_global_device_ids=true | all-gather | bytes 417792 | tf_op jit(solution)/shard_map/all_gather | solution.py:53
  118.6 11.8 %gather_fusion = f32[2048]{0:T(1024)S(1)} fusion(f32[16384]{0:T(1024)S(1)} %copy-done, s32[2048]{0:T(1024)S(1)} %broadcast_clamp_fusion), kind=kCustom, calls=%fused_computation | custom fusion | bytes 24576 | tf_op jit(solution)/shard_map/gather | solution.py:41
  130.5 2.5 reduce_sum.192
  134.0 9.1 %multiply_reduce_fusion.8 = (f32[]{:T(128)}, f32[32,8,256]{2,0,1:T(8,128)S(1)}) fusion(f32[32,8,256]{2,1,0:T(8,128)S(1)} %copy-done.4, f32[8,256]{1,0:T(8,128)S(1)} %reshape.25, f32[32,8,256]{2,1,0:T(8,128)S(1)} %copy-done.3, bf16[8,256,3072]{2,1,0:T(8,128)(2,1)} %copy-done.2, f32[32,3072]{1,0:T(8,128)S(1)} %get-tuple-element.42), kind=kOutput, calls=%fused_computation.47 | convolution fusion | flops 403537920 | bytes 13770756 | tf_op jit(solution)/shard_map/kmu,tu->tkm/dot_general | solution.py:74
  143.1 7.5 %fusion = bf16[32,3072]{1,0:T(8,128)(2,1)} fusion(bf16[8,256,3072]{2,1,0:T(8,128)(2,1)} %copy-done.2, f32[32,8,256]{2,0,1:T(8,128)S(1)} %get-tuple-element.46, f32[32,8,256]{2,1,0:T(8,128)S(1)} %copy-done.3, f32[8,256]{1,0:T(8,128)S(1)} %reshape.25), kind=kOutput, calls=%fused_computation.5 | convolution fusion | flops 403275776 | bytes 13312000 | tf_op jit(solution)/shard_map/tkm,kmu->tu/dot_general | solution.py:63
  152.2 31.3 %all-reduce.9 = (f32[32]{0:T(128)S(1)}, f32[]{:T(128)}) all-reduce(f32[32]{0:T(128)S(1)} %dynamic-update-slice, f32[]{:T(128)} %get-tuple-element.45), channel_id=1, replica_groups=mesh['grp'=2,'ctg'=16] {'ctg'}, use_global_device_ids=true, to_apply=%add.8 | all-reduce | flops 33 | bytes 264
  187.7 5.7 %all-gather.14.cloned.1.call-done = bf16[512,3072]{1,0:T(8,128)(2,1)} async-done(((bf16[32,3072]{1,0:T(8,128)(2,1)}), bf16[512,3072]{1,0:T(8,128)(2,1)}) %all-gather.14.cloned.1.call-update) | async-done | bytes 3145744 | tf_op jit(solution)/shard_map/all_gather | solution.py:64
  193.4 2.5 reduce_sum.198
  196.9 9.1 %multiply_reduce_fusion.7 = (f32[]{:T(128)}, f32[32,8,256]{2,0,1:T(8,128)S(1)}) fusion(f32[32,8,256]{2,0,1:T(8,128)S(1)} %get-tuple-element.46, f32[]{:T(128)S(6)} %mul.251, f32[8,256]{1,0:T(8,128)S(1)} %reshape.25, f32[32,8,256]{2,1,0:T(8,128)S(1)} %copy-done.3, bf16[8,256,3072]{2,1,0:T(8,128)(2,1)} %copy-done.2, f32[32,3072]{1,0:T(8,128)S(1)} %get-tuple-element.36), kind=kOutput, calls=%fused_computation.44 | convolution fusion | flops 403865600 | bytes 13770760 | tf_op jit(solution)/shard_map/kmu,tu->tkm/dot_general | solution.py:74
  205.9 7.5 %fusion.1 = bf16[32,3072]{1,0:T(8,128)(2,1)} fusion(bf16[8,256,3072]{2,1,0:T(8,128)(2,1)} %copy-done.2, f32[32,8,256]{2,0,1:T(8,128)S(1)} %get-tuple-element.48, f32[]{:T(128)S(6)} %mul.251, f32[32,8,256]{2,1,0:T(8,128)S(1)} %copy-done.3, f32[8,256]{1,0:T(8,128)S(1)} %reshape.25), kind=kOutput, calls=%fused_computation.6 | convolution fusion | flops 403275776 | bytes 13312004 | tf_op jit(solution)/shard_map/tkm,kmu->tu/dot_general | solution.py:63
  213.5 32.2 %psum.22 = f32[]{:T(128)} all-reduce(f32[]{:T(128)} %get-tuple-element.47), channel_id=1, replica_groups=mesh['grp'=2,'ctg'=16] {'ctg'}, use_global_device_ids=true, to_apply=%region_9.10 | all-reduce | flops 1 | bytes 8 | tf_op jit(solution)/shard_map/psum | solution.py:82
  249.8 7.8 %all-gather.16.cloned.1.call-done = bf16[512,3072]{1,0:T(8,128)(2,1)} async-done(((bf16[32,3072]{1,0:T(8,128)(2,1)}), bf16[512,3072]{1,0:T(8,128)(2,1)}) %all-gather.16.cloned.1.call-update) | async-done | bytes 3145744 | tf_op jit(solution)/shard_map/all_gather | solution.py:64
  261.1 9.0 %multiply_reduce_fusion.6 = (f32[]{:T(128)}, f32[32,8,256]{2,0,1:T(8,128)S(1)}) fusion(f32[32,8,256]{2,0,1:T(8,128)S(1)} %get-tuple-element.48, f32[]{:T(128)S(6)} %mul.268, f32[]{:T(128)S(6)} %mul.251, f32[8,256]{1,0:T(8,128)S(1)} %reshape.25, f32[32,8,256]{2,1,0:T(8,128)S(1)} %copy-done.3, bf16[8,256,3072]{2,1,0:T(8,128)(2,1)} %copy-done.2, ...), kind=kOutput, calls=%fused_computation.41 | convolution fusion | flops 403865600 | bytes 13770764 | tf_op jit(solution)/shard_map/kmu,tu->tkm/dot_general | solution.py:74
  270.1 7.5 %fusion.2 = bf16[32,3072]{1,0:T(8,128)(2,1)} fusion(bf16[8,256,3072]{2,1,0:T(8,128)(2,1)} %copy-done.2, f32[32,8,256]{2,0,1:T(8,128)S(1)} %get-tuple-element.50, f32[]{:T(128)S(6)} %mul.268, f32[32,8,256]{2,1,0:T(8,128)S(1)} %copy-done.3, f32[8,256]{1,0:T(8,128)S(1)} %reshape.25), kind=kOutput, calls=%fused_computation.7 | convolution fusion | flops 403275776 | bytes 13312004 | tf_op jit(solution)/shard_map/tkm,kmu->tu/dot_general | solution.py:63
  277.7 32.4 %psum.23 = f32[]{:T(128)} all-reduce(f32[]{:T(128)} %get-tuple-element.49), channel_id=1, replica_groups=mesh['grp'=2,'ctg'=16] {'ctg'}, use_global_device_ids=true, to_apply=%region_16.17 | all-reduce | flops 1 | bytes 8 | tf_op jit(solution)/shard_map/psum | solution.py:82
  314.2 7.5 %all-gather.18.cloned.1.call-done = bf16[512,3072]{1,0:T(8,128)(2,1)} async-done(((bf16[32,3072]{1,0:T(8,128)(2,1)}), bf16[512,3072]{1,0:T(8,128)(2,1)}) %all-gather.18.cloned.1.call-update) | async-done | bytes 3145744 | tf_op jit(solution)/shard_map/all_gather | solution.py:64
  324.6 8.4 %multiply_subtract_fusion.7 = f32[32,8,256]{2,0,1:T(8,128)S(1)} fusion(bf16[8,256,3072]{2,1,0:T(8,128)(2,1)} %copy-done.2, f32[32,8,256]{2,0,1:T(8,128)S(1)} %get-tuple-element.50, f32[32,3072]{1,0:T(8,128)S(1)} %get-tuple-element.19, f32[]{:T(128)S(6)} %mul.286, f32[]{:T(128)S(6)} %mul.268, f32[8,256]{1,0:T(8,128)S(1)} %reshape.25, ...), kind=kOutput, calls=%fused_computation.40 | convolution fusion | flops 403668992 | bytes 13770760 | tf_op jit(solution)/shard_map/kmu,tu->tkm/dot_general | solution.py:74
  (79 shorter events, 17.5 us)
Async XLA Ops:
  7.2 111.5 %copy-start = (f32[16384]{0:T(1024)S(1)}, f32[16384]{0:T(1024)}, u32[]{:S(2)}) copy-start(f32[16384]{0:T(1024)} %param.17) | copy-start | bytes 196612
  7.2 123.3 %all-gather.12.cloned.1.call-start = ((), (), s32[]{:S(2)}) async-start(), calls=%async_computation | async-start | bytes 3342336 | tf_op jit(solution)/shard_map/all_gather | solution.py:64
  14.2 19.3 %copy-start.4 = (f32[32,8,256]{2,1,0:T(8,128)S(1)}, f32[32,8,256]{2,1,0:T(8,128)}, u32[]{:S(2)}) copy-start(f32[32,8,256]{2,1,0:T(8,128)} %param.26) | copy-start | bytes 786436
  45.0 4.6 %copy-start.2 = (bf16[8,256,3072]{2,1,0:T(8,128)(2,1)}, bf16[8,256,3072]{2,1,0:T(8,128)(2,1)S(1)}, u32[]{:S(2)}) copy-start(bf16[8,256,3072]{2,1,0:T(8,128)(2,1)S(1)} %mul.234) | copy-start | bytes 37748740
  49.6 3.1 copy-start.10
  49.6 3.1 copy-start.7
  49.6 28.1 %copy-start.8 = (f32[2,3072]{1,0:T(2,128)S(1)}, f32[2,3072]{1,0:T(2,128)}, u32[]{:S(2)}) copy-start(f32[2,3072]{1,0:T(2,128)} %param.27) | copy-start | bytes 73732
  49.6 47.4 %copy-start.9 = (f32[2,3072]{1,0:T(2,128)S(1)}, f32[2,3072]{1,0:T(2,128)}, u32[]{:S(2)}) copy-start(f32[2,3072]{1,0:T(2,128)} %param.25) | copy-start | bytes 73732
  49.6 69.0 %copy-start.12 = (s32[8,256]{1,0:T(8,128)S(1)}, s32[8,256]{1,0:T(8,128)}, u32[]{:S(2)}) copy-start(s32[8,256]{1,0:T(8,128)} %param.16) | copy-start | bytes 24580
  49.6 80.8 %copy-start.5 = (f32[3072]{0:T(1024)S(1)}, f32[3072]{0:T(1024)}, u32[]{:S(2)}) copy-start(f32[3072]{0:T(1024)} %param.20) | copy-start | bytes 36868
  49.6 80.8 %copy-start.11 = (f32[3072]{0:T(1024)S(1)}, f32[3072]{0:T(1024)}, u32[]{:S(2)}) copy-start(f32[3072]{0:T(1024)} %param.21) | copy-start | bytes 36868
  52.6 81.4 %copy-start.3 = (f32[32,8,256]{2,1,0:T(8,128)S(1)}, f32[32,8,256]{2,1,0:T(8,128)}, u32[]{:S(2)}) copy-start(f32[32,8,256]{2,1,0:T(8,128)} %param.18) | copy-start | bytes 786436
  52.6 140.8 %all-gather.14.cloned.1.call-start = ((), (), s32[]{:S(2)}) async-start(), calls=%async_computation.1 | async-start | bytes 3342336 | tf_op jit(solution)/shard_map/all_gather | solution.py:64
  134.0 16.7 %copy-start.6 = (f32[3072]{0:T(1024)S(1)}, f32[3072]{0:T(1024)}, u32[]{:S(2)}) copy-start(f32[3072]{0:T(1024)} %param.22) | copy-start | bytes 36868
  134.0 16.8 %copy-start.14 = (u32[32]{0:T(128)S(1)}, u32[32]{0:T(128)}, u32[]{:S(2)}) copy-start(u32[32]{0:T(128)} %constant.74) | copy-start | bytes 388
  134.0 18.0 %copy-start.13 = (f32[2]{0:T(128)S(1)}, f32[2]{0:T(128)}, u32[]{:S(2)}) copy-start(f32[2]{0:T(128)} %param.24) | copy-start | bytes 28
  150.6 107.0 %all-gather.16.cloned.1.call-start = ((), (), s32[]{:S(2)}) async-start(), calls=%async_computation.2 | async-start | bytes 3342336 | tf_op jit(solution)/shard_map/all_gather | solution.py:64
  213.4 108.3 %all-gather.18.cloned.1.call-start = ((), (), s32[]{:S(2)}) async-start(), calls=%async_computation.3 | async-start | bytes 3342336 | tf_op jit(solution)/shard_map/all_gather | solution.py:64
  270.1 65.0 %copy-start.1 = (f32[16384]{0:T(1024)S(1)}, f32[16384]{0:T(1024)}, u32[]{:S(2)}) copy-start(f32[16384]{0:T(1024)} %param.17) | copy-start | bytes 196612
Sparse Core Ops, SparseCore 0:
  52.7 49.6 all-gather.11
  150.8 42.5 all-gather.13
  213.5 44.0 all-gather.15
  277.8 43.8 all-gather.17
